TPU v7x, 256 devices: a whole 4x4x8 slice. The times are simulated.
256 devices in a mesh: seq: 32 (over z, y), head: 8 (over x, core).
Axes of the slice: x: 4, y: 4, z: 8, core: 2. Of those that a mesh axis runs over, the one named last changes fastest.
Arguments:
- query_in: bfloat16 [32768, 32, 128], P(('seq', 'head')), may hold values from -6 to 6
- key_in: bfloat16 [32768, 32, 128], P(('seq', 'head')), may hold values from -6 to 6
- value_in: bfloat16 [32768, 32, 128], P(('seq', 'head')), may hold values from -6 to 6
- grad_out: bfloat16 [32768, 32, 128], P(('seq', 'head')), may hold values from -6 to 6
- log_decay: bfloat16 [32768, 32], P(('seq', 'head')), may hold values from -1 to 0, as said below
Outputs:
- attended: bfloat16 [32768, 32, 128], P(('seq', 'head'))
- grad_query: bfloat16 [32768, 32, 128], P(('seq', 'head'))
- grad_key: bfloat16 [32768, 32, 128], P(('seq', 'head'))
- grad_value: bfloat16 [32768, 32, 128], P(('seq', 'head'))
Inputs may be any that keep to these rules, and one draw needn't show every extreme that they name: Every entry of log_decay is negative.
All inputs are finite; a program needn't handle non-finite values.
Results may differ from a plain program's by a relative error of at most 0.007.
Values may be sent and summed in bfloat16 or wider, within the bound.
A program may use at most 128 MiB of HBM per device.

v0:
```python
import jax
import jax.numpy as jnp
from jax import lax
from jax.sharding import PartitionSpec as P

precise = lax.Precision.HIGHEST


def shards(query_in, key_in, value_in, grad_out, log_decay):
    f32 = jnp.float32
    bf16 = jnp.bfloat16
    queries, keys_all, values, grads, token_decays = (
        lax.all_to_all(query_in, "head", split_axis=1, concat_axis=0, tiled=True),
        lax.all_to_all(key_in, "head", split_axis=1, concat_axis=0, tiled=True),
        lax.all_to_all(value_in, "head", split_axis=1, concat_axis=0, tiled=True),
        lax.all_to_all(grad_out, "head", split_axis=1, concat_axis=0, tiled=True),
        lax.all_to_all(log_decay, "head", split_axis=1, concat_axis=0, tiled=True),
    )
    segment_length = queries.shape[0]
    width = queries.shape[2]
    scaling = 1.0 / width
    within = jnp.cumsum(token_decays.astype(f32), axis=0)
    seg_total = within[-1]
    to_start = jnp.exp(within)[:, :, None]
    to_end = jnp.exp(seg_total[None, :] - within)[:, :, None]
    keys_end = (keys_all.astype(f32) * to_end).astype(bf16)
    values_end = (values.astype(f32) * to_end).astype(bf16)
    queries_start = (queries.astype(f32) * to_start).astype(bf16)
    grads_start = (grads.astype(f32) * to_start).astype(bf16)
    local_kv = jnp.einsum("thd,the->hde", keys_end, values, preferred_element_type=f32).astype(bf16)
    local_qg = jnp.einsum("thd,the->hde", queries_start, grads, preferred_element_type=f32).astype(
        bf16
    )
    seg_count = lax.axis_size("seq")
    seq_place = lax.axis_index("seq")
    totals = lax.all_gather(seg_total[None, :], "seq", axis=0, tiled=True)
    cum_inc = jnp.cumsum(totals, axis=0)
    cum_exc = cum_inc - totals
    mine_inc = lax.dynamic_index_in_dim(cum_inc, seq_place, 0, keepdims=False)
    mine_exc = lax.dynamic_index_in_dim(cum_exc, seq_place, 0, keepdims=False)
    ranks = jnp.arange(seg_count)[:, None]
    earlier = ranks < seq_place
    later_on = ranks > seq_place
    w_in = jnp.where(earlier, jnp.exp(jnp.where(earlier, mine_exc[None, :] - cum_inc, 0.0)), 0.0)
    w_out = jnp.where(later_on, jnp.exp(jnp.where(later_on, cum_exc - mine_inc[None, :], 0.0)), 0.0)
    new_in = jnp.einsum(
        "ih,ihde->hde",
        w_in,
        lax.all_gather(local_kv[None], "seq", axis=0, tiled=True).astype(f32),
        precision=precise,
    )
    new_out = jnp.einsum(
        "ih,ihde->hde",
        w_out,
        lax.all_gather(local_qg[None], "seq", axis=0, tiled=True).astype(f32),
        precision=precise,
    )
    state_in = new_in
    state_out = new_out
    state_in = state_in.astype(bf16)
    state_out = state_out.astype(bf16)
    head_specific = within.T
    causal = jnp.arange(segment_length)[:, None] >= jnp.arange(segment_length)[None, :]
    decay_mat = jnp.where(
        causal,
        jnp.exp(jnp.where(causal, head_specific[:, :, None] - head_specific[:, None, :], 0.0)),
        0.0,
    )
    scores = jnp.einsum("thd,shd->hts", queries, keys_all, preferred_element_type=f32)
    attn_w = (scaling * scores * decay_mat).astype(bf16)
    intra = jnp.einsum("hts,shd->thd", attn_w, values, preferred_element_type=f32)
    attended = (
        intra
        + scaling * jnp.einsum("thd,hde->the", queries_start, state_in, preferred_element_type=f32)
    ).astype(bf16)
    back_raw = jnp.einsum("the,she->hts", grads, values, preferred_element_type=f32)
    back_w = (scaling * back_raw * decay_mat).astype(bf16)
    grad_query = (
        jnp.einsum("hts,shd->thd", back_w, keys_all, preferred_element_type=f32)
        + scaling * jnp.einsum("the,hde->thd", grads_start, state_in, preferred_element_type=f32)
    ).astype(bf16)
    grad_key = (
        jnp.einsum("hts,thd->shd", back_w, queries, preferred_element_type=f32)
        + scaling * jnp.einsum("she,hde->shd", values_end, state_out, preferred_element_type=f32)
    ).astype(bf16)
    grad_value = (
        jnp.einsum("hts,the->she", attn_w, grads, preferred_element_type=f32)
        + scaling * jnp.einsum("shd,hde->she", keys_end, state_out, preferred_element_type=f32)
    ).astype(bf16)
    results = (
        lax.all_to_all(attended, "head", split_axis=0, concat_axis=1, tiled=True),
        lax.all_to_all(grad_query, "head", split_axis=0, concat_axis=1, tiled=True),
        lax.all_to_all(grad_key, "head", split_axis=0, concat_axis=1, tiled=True),
        lax.all_to_all(grad_value, "head", split_axis=0, concat_axis=1, tiled=True),
    )
    return (results[0], results[1], results[2], results[3])


def solution(mesh):
    return jax.shard_map(
        shards,
        mesh=mesh,
        in_specs=(
            P(("seq", "head"), None, None),
            P(("seq", "head"), None, None),
            P(("seq", "head"), None, None),
            P(("seq", "head"), None, None),
            P(("seq", "head"), None),
        ),
        out_specs=(
            P(("seq", "head"), None, None),
            P(("seq", "head"), None, None),
            P(("seq", "head"), None, None),
            P(("seq", "head"), None, None),
        ),
        check_vma=False,
    )
```

profile of v0, /device:TPU:1, one launch (start us, length us, event | category | flops | bytes accessed | tf_op | source)
XLA Modules:
  0.0 301.6 jit_solution(2192634646455913351)
XLA Ops:
  7.2 6.6 %all-to-all-start.2 = ((bf16[128,8,4]{0,2,1:T(4,128)(2,1)}), bf16[128,8,4]{0,2,1:T(4,128)(2,1)S(1)}, u32[]{:S(2)}, u32[]{:S(2)}) async-start(bf16[128,8,4]{0,2,1:T(4,128)(2,1)} %bitcast.154), calls=%async_computation.2 | async-start | bytes 16384 | tf_op jit(solution)/shard_map/all_to_all | solution.py:17
  18.4 4.2 %all-to-all-start.1 = ((bf16[128,32,128]{2,0,1:T(8,128)(2,1)}), bf16[128,32,128]{2,0,1:T(8,128)(2,1)S(1)}, u32[]{:S(2)}, u32[]{:S(2)}) async-start(bf16[128,32,128]{2,0,1:T(8,128)(2,1)} %copy.120), calls=%async_computation.1 | async-start | bytes 2097152 | tf_op jit(solution)/shard_map/all_to_all | solution.py:14
  24.0 13.7 %all-to-all-done.1 = bf16[128,32,128]{2,0,1:T(8,128)(2,1)S(1)} async-done(((bf16[128,32,128]{2,0,1:T(8,128)(2,1)}), bf16[128,32,128]{2,0,1:T(8,128)(2,1)S(1)}, u32[]{:S(2)}, u32[]{:S(2)}) %all-to-all-start.1) | async-done | bytes 1048608 | tf_op jit(solution)/shard_map/all_to_all | solution.py:14
  37.7 4.3 %all-to-all-start.3 = ((bf16[128,32,128]{2,0,1:T(8,128)(2,1)}), bf16[128,32,128]{2,0,1:T(8,128)(2,1)S(1)}, u32[]{:S(2)}, u32[]{:S(2)}) async-start(bf16[128,32,128]{2,0,1:T(8,128)(2,1)} %copy.122), calls=%async_computation.3 | async-start | bytes 2097152 | tf_op jit(solution)/shard_map/all_to_all | solution.py:15
  44.0 13.1 %all-to-all-done.3 = bf16[128,32,128]{2,0,1:T(8,128)(2,1)S(1)} async-done(((bf16[128,32,128]{2,0,1:T(8,128)(2,1)}), bf16[128,32,128]{2,0,1:T(8,128)(2,1)S(1)}, u32[]{:S(2)}, u32[]{:S(2)}) %all-to-all-start.3) | async-done | bytes 1048608 | tf_op jit(solution)/shard_map/all_to_all | solution.py:15
  62.9 4.3 %all-to-all-start = ((bf16[128,32,128]{2,0,1:T(8,128)(2,1)}), bf16[128,32,128]{2,0,1:T(8,128)(2,1)S(1)}, u32[]{:S(2)}, u32[]{:S(2)}) async-start(bf16[128,32,128]{2,0,1:T(8,128)(2,1)} %copy.118), calls=%async_computation | async-start | bytes 2097152 | tf_op jit(solution)/shard_map/all_to_all | solution.py:13
  68.6 13.7 %all-to-all-done = bf16[128,32,128]{2,0,1:T(8,128)(2,1)S(1)} async-done(((bf16[128,32,128]{2,0,1:T(8,128)(2,1)}), bf16[128,32,128]{2,0,1:T(8,128)(2,1)S(1)}, u32[]{:S(2)}, u32[]{:S(2)}) %all-to-all-start) | async-done | bytes 1048608 | tf_op jit(solution)/shard_map/all_to_all | solution.py:13
  82.3 4.3 %all-to-all-start.5 = ((bf16[128,32,128]{2,0,1:T(8,128)(2,1)}), bf16[128,32,128]{2,0,1:T(8,128)(2,1)S(1)}, u32[]{:S(2)}, u32[]{:S(2)}) async-start(bf16[128,32,128]{2,0,1:T(8,128)(2,1)} %copy.132), calls=%async_computation.5 | async-start | bytes 2097152 | tf_op jit(solution)/shard_map/all_to_all | solution.py:16
  86.8 15.0 %all-to-all-done.5 = bf16[128,32,128]{2,0,1:T(8,128)(2,1)S(1)} async-done(((bf16[128,32,128]{2,0,1:T(8,128)(2,1)}), bf16[128,32,128]{2,0,1:T(8,128)(2,1)S(1)}, u32[]{:S(2)}, u32[]{:S(2)}) %all-to-all-start.5) | async-done | bytes 1048608 | tf_op jit(solution)/shard_map/all_to_all | solution.py:16
  104.2 37.7 %all-gather.2 = f32[32,1,4]{2,1,0:T(1,128)S(1)} all-gather(f32[1,1,4]{2,1,0:T(1,128)S(1)} %bitcast.155), channel_id=1, replica_groups=mesh['seq'=32,'head'=8] {'seq'}, dimensions={0}, use_global_device_ids=true | all-gather | bytes 528 | tf_op jit(solution)/shard_map/all_gather | solution.py:36
  142.4 7.4 %multiply_convert_fusion = bf16[4,1024,1024]{2,1,0:T(8,128)(2,1)S(1)} fusion(bf16[1024,4,128]{2,0,1:T(8,128)(2,1)S(1)} %bitcast.118, bf16[1024,4,128]{2,0,1:T(8,128)(2,1)} %bitcast.139, f32[4,1024]{1,0:T(4,128)S(1)} %bitcast.150, pred[1024,1024]{1,0:T(8,128)(4,1)S(1)} %iota_compare_fusion), kind=kOutput, calls=%fused_computation | convolution fusion | flops 1098907648 | bytes 11550720 | tf_op jit(solution)/shard_map/the,she->hts/dot_general | solution.py:76
  153.8 7.8 %multiply_convert_fusion.1 = bf16[4,1024,1024]{2,1,0:T(8,128)(2,1)} fusion(bf16[1024,4,128]{2,0,1:T(8,128)(2,1)S(1)} %bitcast.122, bf16[1024,4,128]{2,0,1:T(8,128)(2,1)S(1)} %bitcast.136, f32[4,1024]{1,0:T(4,128)S(1)} %bitcast.151, pred[1024,1024]{1,0:T(8,128)(4,1)S(1)} %iota_compare_fusion), kind=kOutput, calls=%fused_computation.1 | convolution fusion | flops 1098907648 | bytes 11550720 | tf_op jit(solution)/shard_map/thd,shd->hts/dot_general | solution.py:69
  161.6 5.8 %fusion = f32[4,1,128,128]{3,1,2,0:T(1,128)S(1)} fusion(f32[32,4,1,1]{0,2,3,1:T(1,128)S(1)} %copy.148, bf16[32,4,128,128]{3,2,1,0:T(8,128)(2,1)} %bitcast.125), kind=kOutput, calls=%fused_computation.4 | convolution fusion | flops 25165824 | bytes 4456960 | tf_op jit(solution)/shard_map/ih,ihde->hde/dot_general | solution.py:46
  170.2 8.2 %all-to-all-start.6 = ((bf16[1024,4,128]{2,1,0:T(4,128)(2,1)}), bf16[1024,4,128]{2,1,0:T(4,128)(2,1)S(1)}, u32[]{:S(2)}, u32[]{:S(2)}) async-start(bf16[1024,4,128]{2,1,0:T(4,128)(2,1)} %copy.135), calls=%async_computation.6 | async-start | bytes 2097152 | tf_op jit(solution)/shard_map/all_to_all | solution.py:92
  178.4 7.7 %fusion.15 = f32[4,1024,128]{2,1,0:T(8,128)} fusion(bf16[4,1024,1024]{2,1,0:T(8,128)(2,1)} %copy-done, bf16[1024,4,128]{2,0,1:T(8,128)(2,1)S(1)} %bitcast.123), kind=kOutput, calls=%fused_computation.44 | convolution fusion | flops 1073741824 | bytes 11534336 | tf_op jit(solution)/shard_map/hts,thd->shd/dot_general | solution.py:83
  186.1 36.4 %all-gather.8.cloned.1.call-done = bf16[128,128,128]{2,1,0:T(8,128)(2,1)} async-done(((bf16[4,128,128]{2,1,0:T(8,128)(2,1)}), bf16[128,128,128]{2,1,0:T(8,128)(2,1)}) %all-gather.8.cloned.1.call-update) | async-done | bytes 4194320 | tf_op jit(solution)/shard_map/all_gather | solution.py:55
  231.8 7.6 %all-to-all-start.7 = ((bf16[1024,4,128]{2,1,0:T(4,128)(2,1)}), bf16[1024,4,128]{2,1,0:T(4,128)(2,1)}, u32[]{:S(2)}, u32[]{:S(2)}) async-start(bf16[1024,4,128]{2,1,0:T(4,128)(2,1)} %copy.141), calls=%async_computation.7 | async-start | bytes 2097152 | tf_op jit(solution)/shard_map/all_to_all | solution.py:93
  239.3 5.9 %fusion.13 = f32[4,1024,128]{2,1,0:T(8,128)S(1)} fusion(bf16[4,1024,1024]{2,1,0:T(8,128)(2,1)} %multiply_convert_fusion.1, bf16[1024,4,128]{2,0,1:T(8,128)(2,1)} %bitcast.141), kind=kOutput, calls=%fused_computation.42 | convolution fusion | flops 1073741824 | bytes 11534336 | tf_op jit(solution)/shard_map/hts,shd->thd/dot_general | solution.py:71
  248.1 6.5 %all-to-all-done.7 = bf16[1024,4,128]{2,1,0:T(4,128)(2,1)} async-done(((bf16[1024,4,128]{2,1,0:T(4,128)(2,1)}), bf16[1024,4,128]{2,1,0:T(4,128)(2,1)}, u32[]{:S(2)}, u32[]{:S(2)}) %all-to-all-start.7) | async-done | bytes 1048608 | tf_op jit(solution)/shard_map/all_to_all | solution.py:93
  254.5 4.3 %all-to-all-start.4 = ((bf16[1024,4,128]{2,1,0:T(4,128)(2,1)}), bf16[1024,4,128]{2,1,0:T(4,128)(2,1)S(1)}, u32[]{:S(2)}, u32[]{:S(2)}) async-start(bf16[1024,4,128]{2,1,0:T(4,128)(2,1)} %copy.130), calls=%async_computation.4 | async-start | bytes 2097152 | tf_op jit(solution)/shard_map/all_to_all | solution.py:91
  258.9 6.4 %fusion.16 = f32[4,1024,128]{2,1,0:T(8,128)S(1)} fusion(bf16[4,1024,1024]{2,1,0:T(8,128)(2,1)} %multiply_convert_fusion.1, bf16[1024,4,128]{2,0,1:T(8,128)(2,1)S(1)} %bitcast.120), kind=kOutput, calls=%fused_computation.45 | convolution fusion | flops 1073741824 | bytes 11534336 | tf_op jit(solution)/shard_map/hts,the->she/dot_general | solution.py:87
  268.1 5.9 %all-to-all-done.4 = bf16[1024,4,128]{2,1,0:T(4,128)(2,1)S(1)} async-done(((bf16[1024,4,128]{2,1,0:T(4,128)(2,1)}), bf16[1024,4,128]{2,1,0:T(4,128)(2,1)S(1)}, u32[]{:S(2)}, u32[]{:S(2)}) %all-to-all-start.4) | async-done | bytes 1048608 | tf_op jit(solution)/shard_map/all_to_all | solution.py:91
  274.0 4.3 %all-to-all-start.8 = ((bf16[1024,4,128]{2,1,0:T(4,128)(2,1)}), bf16[1024,4,128]{2,1,0:T(4,128)(2,1)S(1)}, u32[]{:S(2)}, u32[]{:S(2)}) async-start(bf16[1024,4,128]{2,1,0:T(4,128)(2,1)} %copy.145), calls=%async_computation.8 | async-start | bytes 2097152 | tf_op jit(solution)/shard_map/all_to_all | solution.py:94
  283.5 9.9 %all-to-all-done.8 = bf16[1024,4,128]{2,1,0:T(4,128)(2,1)S(1)} async-done(((bf16[1024,4,128]{2,1,0:T(4,128)(2,1)}), bf16[1024,4,128]{2,1,0:T(4,128)(2,1)S(1)}, u32[]{:S(2)}, u32[]{:S(2)}) %all-to-all-start.8) | async-done | bytes 1048608 | tf_op jit(solution)/shard_map/all_to_all | solution.py:94
  (71 shorter events, 46.1 us)
Async XLA Ops:
  7.2 15.4 %copy-start.6 = (bf16[128,32,128]{2,1,0:T(8,128)(2,1)S(1)}, bf16[128,32,128]{2,1,0:T(8,128)(2,1)}, u32[]{:S(2)}) copy-start(bf16[128,32,128]{2,1,0:T(8,128)(2,1)} %param.7) | copy-start | bytes 3145732
  7.2 11.3 %all-to-all-start.2 = ((bf16[128,8,4]{0,2,1:T(4,128)(2,1)}), bf16[128,8,4]{0,2,1:T(4,128)(2,1)S(1)}, u32[]{:S(2)}, u32[]{:S(2)}) async-start(bf16[128,8,4]{0,2,1:T(4,128)(2,1)} %bitcast.154), calls=%async_computation.2 | async-start | bytes 16384 | tf_op jit(solution)/shard_map/all_to_all | solution.py:17
  18.4 19.3 %all-to-all-start.1 = ((bf16[128,32,128]{2,0,1:T(8,128)(2,1)}), bf16[128,32,128]{2,0,1:T(8,128)(2,1)S(1)}, u32[]{:S(2)}, u32[]{:S(2)}) async-start(bf16[128,32,128]{2,0,1:T(8,128)(2,1)} %copy.120), calls=%async_computation.1 | async-start | bytes 2097152 | tf_op jit(solution)/shard_map/all_to_all | solution.py:14
  37.7 19.5 %all-to-all-start.3 = ((bf16[128,32,128]{2,0,1:T(8,128)(2,1)}), bf16[128,32,128]{2,0,1:T(8,128)(2,1)S(1)}, u32[]{:S(2)}, u32[]{:S(2)}) async-start(bf16[128,32,128]{2,0,1:T(8,128)(2,1)} %copy.122), calls=%async_computation.3 | async-start | bytes 2097152 | tf_op jit(solution)/shard_map/all_to_all | solution.py:15
  42.0 119.5 %all-gather.6.cloned.1.call-start = ((), (), s32[]{:S(2)}) async-start(), calls=%async_computation.9 | async-start | bytes 4325376 | tf_op jit(solution)/shard_map/all_gather | solution.py:49
  43.9 123.5 %copy-start.8 = (f32[1024,4]{0,1:T(4,128)}, f32[1024,4]{0,1:T(4,128)S(1)}, u32[]{:S(2)}) copy-start(f32[1024,4]{0,1:T(4,128)S(1)} %get-tuple-element.7) | copy-start | bytes 49156
  44.0 18.8 %copy-start.1 = (bf16[128,8,4,128]{3,0,1,2:T(8,128)(2,1)}, bf16[128,8,4,128]{3,0,1,2:T(8,128)(2,1)S(1)}, u32[]{:S(2)}) copy-start(bf16[128,8,4,128]{3,0,1,2:T(8,128)(2,1)S(1)} %copy.121) | copy-start | bytes 3145732
  57.3 1.0 copy-start.4
  57.3 9.9 %copy-start.7 = (bf16[128,32,128]{2,1,0:T(8,128)(2,1)S(1)}, bf16[128,32,128]{2,1,0:T(8,128)(2,1)}, u32[]{:S(2)}) copy-start(bf16[128,32,128]{2,1,0:T(8,128)(2,1)} %param.8) | copy-start | bytes 3145732
  62.9 19.5 %all-to-all-start = ((bf16[128,32,128]{2,0,1:T(8,128)(2,1)}), bf16[128,32,128]{2,0,1:T(8,128)(2,1)S(1)}, u32[]{:S(2)}, u32[]{:S(2)}) async-start(bf16[128,32,128]{2,0,1:T(8,128)(2,1)} %copy.118), calls=%async_computation | async-start | bytes 2097152 | tf_op jit(solution)/shard_map/all_to_all | solution.py:13
  82.3 19.5 %all-to-all-start.5 = ((bf16[128,32,128]{2,0,1:T(8,128)(2,1)}), bf16[128,32,128]{2,0,1:T(8,128)(2,1)S(1)}, u32[]{:S(2)}, u32[]{:S(2)}) async-start(bf16[128,32,128]{2,0,1:T(8,128)(2,1)} %copy.132), calls=%async_computation.5 | async-start | bytes 2097152 | tf_op jit(solution)/shard_map/all_to_all | solution.py:16
  86.6 135.9 %all-gather.8.cloned.1.call-start = ((), (), s32[]{:S(2)}) async-start(), calls=%async_computation.10 | async-start | bytes 4325376 | tf_op jit(solution)/shard_map/all_gather | solution.py:55
  142.4 7.4 %copy-start.2 = (bf16[128,8,4,128]{3,0,1,2:T(8,128)(2,1)S(1)}, bf16[128,8,4,128]{3,0,1,2:T(8,128)(2,1)}, u32[]{:S(2)}) copy-start(bf16[128,8,4,128]{3,0,1,2:T(8,128)(2,1)} %copy-done.1) | copy-start | bytes 3145732
  149.8 4.0 %copy-start = (bf16[4,1024,1024]{2,1,0:T(8,128)(2,1)}, bf16[4,1024,1024]{2,1,0:T(8,128)(2,1)S(1)}, u32[]{:S(2)}) copy-start(bf16[4,1024,1024]{2,1,0:T(8,128)(2,1)S(1)} %multiply_convert_fusion) | copy-start | bytes 25165828
  161.6 5.9 %copy-start.5 = (f32[4,1024,128]{2,1,0:T(8,128)S(1)}, f32[4,1024,128]{2,1,0:T(8,128)}, u32[]{:S(2)}) copy-start(f32[4,1024,128]{2,1,0:T(8,128)} %fusion.14) | copy-start | bytes 6291460
  170.2 61.5 %all-to-all-start.6 = ((bf16[1024,4,128]{2,1,0:T(4,128)(2,1)}), bf16[1024,4,128]{2,1,0:T(4,128)(2,1)S(1)}, u32[]{:S(2)}, u32[]{:S(2)}) async-start(bf16[1024,4,128]{2,1,0:T(4,128)(2,1)} %copy.135), calls=%async_computation.6 | async-start | bytes 2097152 | tf_op jit(solution)/shard_map/all_to_all | solution.py:92
  231.8 22.8 %all-to-all-start.7 = ((bf16[1024,4,128]{2,1,0:T(4,128)(2,1)}), bf16[1024,4,128]{2,1,0:T(4,128)(2,1)}, u32[]{:S(2)}, u32[]{:S(2)}) async-start(bf16[1024,4,128]{2,1,0:T(4,128)(2,1)} %copy.141), calls=%async_computation.7 | async-start | bytes 2097152 | tf_op jit(solution)/shard_map/all_to_all | solution.py:93
  239.3 6.0 %copy-start.9 = (f32[1024,4]{0,1:T(4,128)S(1)}, f32[1024,4]{0,1:T(4,128)}, u32[]{:S(2)}) copy-start(f32[1024,4]{0,1:T(4,128)} %copy-done.8) | copy-start | bytes 49156
  254.5 19.5 %all-to-all-start.4 = ((bf16[1024,4,128]{2,1,0:T(4,128)(2,1)}), bf16[1024,4,128]{2,1,0:T(4,128)(2,1)S(1)}, u32[]{:S(2)}, u32[]{:S(2)}) async-start(bf16[1024,4,128]{2,1,0:T(4,128)(2,1)} %copy.130), calls=%async_computation.4 | async-start | bytes 2097152 | tf_op jit(solution)/shard_map/all_to_all | solution.py:91
  258.9 6.4 %copy-start.3 = (bf16[128,8,4,128]{3,0,1,2:T(8,128)(2,1)S(1)}, bf16[128,8,4,128]{3,0,1,2:T(8,128)(2,1)}, u32[]{:S(2)}) copy-start(bf16[128,8,4,128]{3,0,1,2:T(8,128)(2,1)} %copy-done.1) | copy-start | bytes 3145732
  274.0 19.4 %all-to-all-start.8 = ((bf16[1024,4,128]{2,1,0:T(4,128)(2,1)}), bf16[1024,4,128]{2,1,0:T(4,128)(2,1)S(1)}, u32[]{:S(2)}, u32[]{:S(2)}) async-start(bf16[1024,4,128]{2,1,0:T(4,128)(2,1)} %copy.145), calls=%async_computation.8 | async-start | bytes 2097152 | tf_op jit(solution)/shard_map/all_to_all | solution.py:94
Sparse Core Ops, SparseCore 0:
  60.4 79.9 all-gather.5
  143.5 78.9 all-gather.7
where the time goes:
time: 302 us
  waiting for transfers between devices  116 us (38%)
  matrix products  54.6 us (18%)
  starting transfers between devices  48.2 us (16%)
  blocking collectives  37.7 us (12%)
  local copies, waits for them, and re-layouts  24.7 us (8%)
  between operations  14.3 us (5%)
  other arithmetic  5.77 us (2%)
    all_gather x1, blocking collectives, shards(): totals = lax.all_gather(seg_total[None, :], 'seq', axis=0, tiled=True)  37.7 us
    all_gather x1, waiting for transfers between devices, shards(): lax.all_gather(local_qg[None], 'seq', axis=0, tiled=True).astype(f32)  36.4 us
    all_to_all x1, waiting for transfers between devices, shards(): lax.all_to_all(grad_out, 'head', split_axis=1, concat_axis=0, tiled=True)  15 us
    all_to_all x1, waiting for transfers between devices, shards(): lax.all_to_all(key_in, 'head', split_axis=1, concat_axis=0, tiled=True)  13.7 us
    all_to_all x1, waiting for transfers between devices, shards(): lax.all_to_all(query_in, 'head', split_axis=1, concat_axis=0, tiled=True)  13.7 us
    all_to_all x1, waiting for transfers between devices, shards(): lax.all_to_all(value_in, 'head', split_axis=1, concat_axis=0, tiled=True)  13.1 us
    all_to_all x1, waiting for transfers between devices, shards(): lax.all_to_all(grad_value, 'head', split_axis=0, concat_axis=1, tiled=True)  9.9 us
    unnamed x27, local copies, waits for them, and re-layouts  9.06 us
  transfers between devices with their start and end apart: 11, of which 9 were waited for; matrix products, arithmetic and copies ran while one was open for 27% of the time, Pallas kernels for 0%

commit v1 on v0

v1 whole, which is shorter than its diff:
```python
import functools

import jax
import jax.numpy as jnp
from jax import lax
from jax.experimental import pallas as pl
from jax.experimental.pallas import tpu as pltpu
from jax.sharding import PartitionSpec as P

MESH = pl.DeviceIdType.MESH
bf16 = jnp.bfloat16
f32 = jnp.float32
NN = (((1,), (0,)), ((), ()))
NT = (((1,), (1,)), ((), ()))
TN = (((0,), (0,)), ((), ()))
PAIRS, NX, NB, NS, ROWS = 16, 4, 2, 32, 16


def dot(a, b, dims=NN):
    return lax.dot_general(a, b, dims, preferred_element_type=f32)


def drain(ref, sem):
    pltpu.make_async_copy(ref, ref, sem).wait()


def kernel(
    l_ref, q_hbm, k_hbm, v_hbm, g_hbm, o_att, o_gq, o_gk, o_gv,
    inb, outb, acc, es_t, ee_t, lf, upper, mask, s_own, s_send, s_recv, c_buf, x_recv, y_send, y_recv,
    z_send, w_recv, d_buf, in_buf, p_send, fin, t_core, t_x, t_y, w_tab, x_tab, f_tab,
    in_sem, out_sem, tc_s, tc_r, tx_s, tx_r, ty_s, ty_r, cu_s, cu_r, xu_s, xu_r, yu_s, yu_r,
    yd_s, yd_r, xd_s, xd_r, cd_s, cd_r,
):
    seg = lax.axis_index("seq")
    head = lax.axis_index("head")
    chip, core = head // 2, head % 2
    other = 1 - core
    partner = {"head": chip * 2 + other}
    scaling = 1.0 / 128
    sources = (q_hbm, k_hbm, v_hbm, g_hbm)
    targets = (o_att, o_gq, o_gk, o_gv)

    def ring(d):
        return lax.rem(chip + d, NX)

    barrier = pltpu.get_barrier_semaphore()
    pl.semaphore_signal(barrier, inc=1, device_id=partner, device_id_type=MESH)
    for d in range(1, NX):
        pl.semaphore_signal(barrier, inc=1, device_id={"head": ring(d) * 2 + core}, device_id_type=MESH)

    def greet(i, _):
        pl.semaphore_signal(barrier, inc=1, device_id={"seq": lax.rem(seg + i, NS)}, device_id_type=MESH)
        return 0

    lax.fori_loop(1, NS, greet, 0)

    def load(n, _):
        side = (n // 4) % 2
        half = other + side * (core - other)
        pair = half * 8 + (n // 8) * 4 + n % 4
        for a in range(4):
            pltpu.make_async_copy(sources[a].at[:, pair], inb.at[pair, a], in_sem.at[pair]).start()
        return 0

    lax.fori_loop(0, PAIRS, load, 0)

    logs = l_ref[...]
    lf[...] = logs.astype(f32)
    padded = jnp.concatenate([logs, jnp.zeros((96, 128), bf16)], axis=0)
    t_core[core] = dot(jnp.ones((8, 128), bf16), padded, NT)
    row2 = lax.broadcasted_iota(jnp.int32, (256, 256), 0)
    col2 = lax.broadcasted_iota(jnp.int32, (256, 256), 1)
    mask[...] = jnp.where((row2 % 2 == col2 % 2) & (row2 >= col2), scaling, 0.0)
    upper[...] = jnp.where(
        lax.broadcasted_iota(jnp.int32, (128, 256), 0) > lax.broadcasted_iota(jnp.int32, (128, 256), 1) // 2, 1.0, 0.0
    ).astype(bf16)
    row = lax.broadcasted_iota(jnp.int32, (256, 128), 0)
    lane = lax.broadcasted_iota(jnp.int32, (256, 128), 1)
    odd = row % 2 == 1
    upto = lane <= row // 2
    ones = jnp.ones((128, 128), bf16)

    def log_rows(pair):
        return jnp.where(odd, lf[pl.ds(2 * pair + 1, 1), :], lf[pl.ds(2 * pair, 1), :])

    def per_head(line):
        r = lax.broadcasted_iota(jnp.int32, (32, 128), 0)
        c = lax.broadcasted_iota(jnp.int32, (32, 128), 1)
        total = jnp.sum(jnp.where(r == c, line, 0.0), axis=1, keepdims=True)
        return jnp.broadcast_to(jnp.exp(total), (32, 128))

    def inputs(pair):
        return [inb.at[pair, a].reshape(256, 128)[...] for a in range(4)]

    def local_state(pair):
        drain(inb.at[pair], in_sem.at[pair])
        q, k, v, g = inputs(pair)
        whole = log_rows(pair)
        es = jnp.exp(dot(jnp.where(upto, whole, 0.0).astype(bf16), ones))
        ee = jnp.exp(dot(jnp.where(upto, 0.0, whole).astype(bf16), ones))
        es_t[pair] = es
        ee_t[pair] = ee

        def split(x):
            return jnp.concatenate([jnp.where(odd, 0.0, x), jnp.where(odd, x, 0.0)], axis=1).astype(bf16)

        return dot(k, split(v.astype(f32) * ee), TN), dot(q, split(g.astype(f32) * es), TN)

    def states(b):
        def theirs(i, _):
            for kind, s in enumerate(local_state(other * 8 + b * 4 + i)):
                s_send[b, i, kind, 0:128, :] = s[:, 0:128].astype(bf16)
                s_send[b, i, kind, 128:256, :] = s[:, 128:256].astype(bf16)
            return 0

        lax.fori_loop(0, 4, theirs, 0)
        up = pltpu.make_async_remote_copy(
            s_send.at[b], s_recv.at[b], cu_s.at[b], cu_r.at[b], device_id=partner, device_id_type=MESH
        )
        up.start()

        def mine(i, _):
            for kind, s in enumerate(local_state(core * 8 + b * 4 + i)):
                s_own[b, i, kind, 0:128, :] = s[:, 0:128]
                s_own[b, i, kind, 128:256, :] = s[:, 128:256]
            return 0

        lax.fori_loop(0, 4, mine, 0)

    def chip_states(b):
        drain(s_recv.at[b], cu_r.at[b])

        def one(i, _):
            for kind in range(2):
                for hd in range(2):
                    at = pl.ds(2 * (core * 8 + b * 4 + i) + hd, 1)
                    r = pl.ds(hd * 128, 128)
                    c_buf[b, i, kind, r, :] = (
                        w_tab[2 * kind, at, :] * s_own[b, i, kind, r, :]
                        + w_tab[2 * kind + 1, at, :] * s_recv[b, i, kind, r, :].astype(f32)
                    ).astype(bf16)
            return 0

        lax.fori_loop(0, 4, one, 0)
        for d in range(1, NX):
            pltpu.make_async_remote_copy(
                c_buf.at[b, ring(d)], x_recv.at[b, chip], xu_s.at[b], xu_r.at[b],
                device_id={"head": ring(d) * 2 + core}, device_id_type=MESH,
            ).start()
        x_recv[b, chip] = c_buf[b, chip]

    def seg_states(b):
        drain(x_recv.at[b, pl.ds(0, 3)], xu_r.at[b])
        pair = core * 8 + b * 4 + chip
        for hd in range(2):
            at = pl.ds(2 * pair + hd, 1)
            r = pl.ds(hd * 128, 128)
            kv = x_recv[b, 0, 0, r, :].astype(f32)
            qg = x_recv[b, 3, 1, r, :].astype(f32)
            for i in range(1, NX):
                kv = kv * x_tab[i, at, :] + x_recv[b, i, 0, r, :].astype(f32)
                qg = qg * x_tab[3 - i, at, :] + x_recv[b, 3 - i, 1, r, :].astype(f32)
            y_send[b, r, :] = kv.astype(bf16)
            y_send[b, pl.ds(256 + hd * 128, 128), :] = qg.astype(bf16)

        def send(i, _):
            to = lax.rem(seg + i, NS)
            pltpu.make_async_remote_copy(
                y_send.at[b, pl.ds(pl.multiple_of(to * ROWS, ROWS), ROWS)], y_recv.at[b, seg], yu_s.at[b], yu_r.at[b],
                device_id={"seq": to}, device_id_type=MESH,
            ).start()
            return 0

        lax.fori_loop(1, NS, send, 0)
        y_recv[b, seg] = y_send[b, pl.ds(pl.multiple_of(seg * ROWS, ROWS), ROWS), :]

    def scan_segments(b):
        drain(y_recv.at[b, pl.ds(0, NS - 1)], yu_r.at[b])
        back = seg // 16

        def step(i, total):
            j = i + back * (31 - 2 * i)
            z_send[b, j] = total.astype(bf16)
            return total * f_tab[b, pl.ds(j, 1), :] + y_recv[b, j].astype(f32)

        lax.fori_loop(0, NS, step, jnp.zeros((ROWS, 128), f32), unroll=4)

        def send(i, _):
            to = lax.rem(seg + i, NS)
            pltpu.make_async_remote_copy(
                z_send.at[b, to], w_recv.at[b, pl.ds(pl.multiple_of(seg * ROWS, ROWS), ROWS)], yd_s.at[b], yd_r.at[b],
                device_id={"seq": to}, device_id_type=MESH,
            ).start()
            return 0

        lax.fori_loop(1, NS, send, 0)
        w_recv[b, pl.ds(pl.multiple_of(seg * ROWS, ROWS), ROWS), :] = z_send[b, seg]

    def chip_entries(b):
        drain(w_recv.at[b, pl.ds(0, (NS - 1) * ROWS)], yd_r.at[b])
        pair = core * 8 + b * 4 + chip
        for hd in range(2):
            at = pl.ds(2 * pair + hd, 1)
            r = pl.ds(hd * 128, 128)
            kv = w_recv[b, r, :].astype(f32)
            qg = w_recv[b, pl.ds(256 + hd * 128, 128), :].astype(f32)
            for i in range(NX):
                d_buf[b, i, 0, r, :] = kv.astype(bf16)
                d_buf[b, 3 - i, 1, r, :] = qg.astype(bf16)
                if i < NX - 1:
                    kv = kv * x_tab[i, at, :] + x_recv[b, i, 0, r, :].astype(f32)
                    qg = qg * x_tab[3 - i, at, :] + x_recv[b, 3 - i, 1, r, :].astype(f32)
        for d in range(1, NX):
            pltpu.make_async_remote_copy(
                d_buf.at[b, ring(d)], in_buf.at[b, chip], xd_s.at[b], xd_r.at[b],
                device_id={"head": ring(d) * 2 + core}, device_id_type=MESH,
            ).start()
        in_buf[b, chip] = d_buf[b, chip]

    def core_entries(b):
        drain(in_buf.at[b, pl.ds(0, 3)], xd_r.at[b])
        first = (1 - core).astype(f32)
        second = core.astype(f32)

        def one(i, _):
            for kind in range(2):
                for hd in range(2):
                    at = pl.ds(2 * (core * 8 + b * 4 + i) + hd, 1)
                    r = pl.ds(hd * 128, 128)
                    entry = in_buf[b, i, kind, r, :].astype(f32)
                    use_mine, use_theirs = (second, first) if kind == 0 else (first, second)
                    tab = 2 - 2 * kind
                    fin[core, b, i, kind, r, :] = (
                        entry * w_tab[tab, at, :] + use_mine * s_recv[b, i, kind, r, :].astype(f32)
                    ).astype(bf16)
                    p_send[b, i, kind, r, :] = (
                        entry * w_tab[tab + 1, at, :] + use_theirs * s_own[b, i, kind, r, :]
                    ).astype(bf16)
            return 0

        lax.fori_loop(0, 4, one, 0)
        pltpu.make_async_remote_copy(
            p_send.at[b], fin.at[core, b], cd_s.at[b], cd_r.at[b], device_id=partner, device_id_type=MESH
        ).start()

    def intra(pair, _):
        q, k, v, g = inputs(pair)
        logs_to = jnp.where(upto, log_rows(pair), 0.0).astype(bf16)
        decay = jnp.exp(dot(logs_to, upper[...])) * mask[...]
        attn = (dot(q, k, NT) * decay).astype(bf16)
        back = (dot(g, v, NT) * decay).astype(bf16)
        acc[pair, 0] = dot(attn, v)
        acc[pair, 1] = dot(back, k)
        acc[pair, 2] = dot(back, q, TN)
        acc[pair, 3] = dot(attn, g, TN)
        return 0

    def finish(half, b):
        def one(i, _):
            pair = half * 8 + b * 4 + i
            q, k, v, g = inputs(pair)
            es = es_t[pair] * scaling
            ee = ee_t[pair] * scaling
            si = fin[half, b, i, 0]
            so = fin[half, b, i, 1]

            def pick(x):
                return jnp.where(odd, x[:, 128:256], x[:, 0:128])

            def put(a, scale, x):
                outb.at[pair, a].reshape(256, 128)[...] = (acc[pair, a] + scale * x).astype(bf16)
                pltpu.make_async_copy(outb.at[pair, a], targets[a].at[:, pair], out_sem.at[pair]).start()

            put(0, es, jnp.where(odd, dot(q, si[128:256]), dot(q, si[0:128])))
            put(1, es, pick(dot(g, si, NT)))
            put(2, ee, pick(dot(v, so, NT)))
            put(3, ee, jnp.where(odd, dot(k, so[128:256]), dot(k, so[0:128])))
            return 0

        lax.fori_loop(0, 4, one, 0)

    pl.semaphore_wait(barrier, NX + NS - 1)
    pltpu.make_async_remote_copy(
        t_core.at[core], t_core.at[core], tc_s, tc_r, device_id=partner, device_id_type=MESH
    ).start()

    states(0)
    drain(t_core.at[0], tc_r)
    t0, t1 = t_core[0], t_core[1]
    e0, e1 = per_head(t0[0:1]), per_head(t1[0:1])
    one_tab = jnp.ones_like(e0)
    w_tab[0] = jnp.where(core == 0, e1, one_tab)
    w_tab[1] = jnp.where(core == 0, one_tab, e1)
    w_tab[2] = jnp.where(core == 0, one_tab, e0)
    w_tab[3] = jnp.where(core == 0, e0, one_tab)
    t_x[chip] = t0 + t1
    for d in range(1, NX):
        pltpu.make_async_remote_copy(
            t_x.at[chip], t_x.at[chip], tx_s, tx_r, device_id={"head": ring(d) * 2 + core}, device_id_type=MESH
        ).start()
    chip_states(0)
    states(1)
    drain(t_x.at[pl.ds(0, 3)], tx_r)
    for i in range(NX):
        x_tab[i] = per_head(t_x[i, 0:1, :])
    t_y[seg] = t_x[0] + t_x[1] + t_x[2] + t_x[3]

    def tell(i, _):
        pltpu.make_async_remote_copy(
            t_y.at[seg], t_y.at[seg], ty_s, ty_r, device_id={"seq": lax.rem(seg + i, NS)}, device_id_type=MESH
        ).start()
        return 0

    lax.fori_loop(1, NS, tell, 0)
    chip_states(1)
    lax.fori_loop(0, 8, intra, 0)
    seg_states(0)
    drain(t_y.at[pl.ds(0, NS - 1)], ty_r)
    seg_logs = t_y[:, 0, :]
    for b in range(NB):
        mine = 2 * (core * 8 + b * 4 + chip) + (seg % 16) // 8
        lanes = lax.broadcasted_iota(jnp.int32, (NS, 128), 1)
        total = jnp.sum(jnp.where(lanes == mine, seg_logs, 0.0), axis=1, keepdims=True)
        f_tab[b] = jnp.broadcast_to(jnp.exp(total), (NS, 128))
    seg_states(1)
    scan_segments(0)
    lax.fori_loop(8, 16, intra, 0)
    scan_segments(1)
    for b in range(NB):
        chip_entries(b)
    for b in range(NB):
        core_entries(b)
        finish(core, b)
        drain(fin.at[other, b], cd_r.at[b])
        finish(other, b)

    drain(t_core.at[0], tc_s)
    drain(t_x.at[pl.ds(0, 3)], tx_s)
    drain(t_y.at[pl.ds(0, NS - 1)], ty_s)
    for b in range(NB):
        drain(s_send.at[b], cu_s.at[b])
        drain(c_buf.at[b, pl.ds(0, 3)], xu_s.at[b])
        drain(y_recv.at[b, pl.ds(0, NS - 1)], yu_s.at[b])
        drain(z_send.at[b, pl.ds(0, NS - 1)], yd_s.at[b])
        drain(d_buf.at[b, pl.ds(0, 3)], xd_s.at[b])
        drain(p_send.at[b], cd_s.at[b])

    def written(pair, _):
        drain(outb.at[pair], out_sem.at[pair])
        return 0

    lax.fori_loop(0, PAIRS, written, 0)


def shards(query_in, key_in, value_in, grad_out, log_decay):
    def paired(x):
        return x.reshape(128, PAIRS, 2, 128)

    vm, dma = pltpu.VMEM, pltpu.SemaphoreType.DMA
    five = (NB, 4, 2, 256, 128)
    scratch = [
        vm((PAIRS, 4, 128, 2, 128), bf16), vm((PAIRS, 4, 128, 2, 128), bf16), vm((PAIRS, 4, 256, 128), f32),
        vm((PAIRS, 256, 128), f32), vm((PAIRS, 256, 128), f32), vm((32, 128), f32), vm((128, 256), bf16),
        vm((256, 256), f32), vm(five, f32), vm(five, bf16), vm(five, bf16), vm(five, bf16), vm(five, bf16),
        vm((NB, 512, 128), bf16), vm((NB, NS, ROWS, 128), bf16), vm((NB, NS, ROWS, 128), bf16),
        vm((NB, 512, 128), bf16), vm(five, bf16), vm(five, bf16), vm(five, bf16), vm((2,) + five, bf16),
        vm((2, 8, 128), f32), vm((NX, 8, 128), f32), vm((NS, 8, 128), f32),
        vm((4, 32, 128), f32), vm((NX, 32, 128), f32), vm((NB, NS, 128), f32),
        dma((PAIRS,)), dma((PAIRS,)), dma, dma, dma, dma, dma, dma,
    ] + [dma((NB,))] * 12
    outs = pl.pallas_call(
        kernel,
        out_shape=[jax.ShapeDtypeStruct((128, PAIRS, 2, 128), bf16)] * 4,
        in_specs=[pl.BlockSpec(memory_space=pltpu.VMEM)] + [pl.BlockSpec(memory_space=pl.ANY)] * 4,
        out_specs=[pl.BlockSpec(memory_space=pl.ANY)] * 4,
        scratch_shapes=scratch,
        compiler_params=pltpu.CompilerParams(collective_id=0, has_side_effects=True, vmem_limit_bytes=60 << 20),
    )(log_decay.T, paired(query_in), paired(key_in), paired(value_in), paired(grad_out))
    return tuple(x.reshape(128, 32, 128) for x in outs)


def solution(mesh):
    spec = P(("seq", "head"), None, None)
    return jax.shard_map(
        shards,
        mesh=mesh,
        in_specs=(spec,) * 4 + (P(("seq", "head"), None),),
        out_specs=(spec,) * 4,
        check_vma=False,
    )
```

time: 302 us -> 65.7 us (0.22)
  waiting for transfers between devices: 116 us -> 0 us
  Pallas kernels: 0 us -> 58.2 us
  matrix products: 54.6 us -> 0 us
  starting transfers between devices: 48.2 us -> 0 us
  blocking collectives: 37.7 us -> 0 us
  local copies, waits for them, and re-layouts: 24.7 us -> 6.53 us
  between operations: 14.3 us -> 0.65 us
  other arithmetic: 5.77 us -> 0 us
    all_to_all x9 -> x0, waiting for transfers between devices: 79.9 us -> none  [the longest x1 15 us: shards(): lax.all_to_all(grad_out, 'head', split_axis=1, concat_axis=0, tiled=True)]
    pallas_call x0 -> x1, Pallas kernels: none -> 58.2 us  [shards(): pl.pallas_call(kernel, out_shape=[jax.ShapeDtypeStruct((128, PAIRS, 2, 12...]
    dot_general x13 -> x0, matrix products: 54.6 us -> none  [the longest x1 7.77 us: shards(): jnp.einsum('thd,shd->hts', queries, keys_all, preferred_element_type=f32)]
    all_to_all x9 -> x0, starting transfers between devices: 48.2 us -> none  [the longest x1 8.2 us: shards(): lax.all_to_all(grad_query, 'head', split_axis=0, concat_axis=1, tiled=True)]
    all_gather x1 -> x0, blocking collectives: 37.7 us -> none  [shards(): totals = lax.all_gather(seg_total[None, :], 'seq', axis=0, tiled=True)]
    all_gather x2 -> x0, waiting for transfers between devices: 36.4 us -> none  [the longest x1 36.4 us: shards(): lax.all_gather(local_qg[None], 'seq', axis=0, tiled=True).astype(f32)]
    convert_element_type x4 -> x0, local copies, waits for them, and re-layouts: 7.13 us -> none  [the longest x1 1.79 us: shards(): grad_value = (jnp.einsum('hts,the->she', attn_w, grads, preferred_element...]
    all_to_all x8 -> x0, local copies, waits for them, and re-layouts: 6.94 us -> none  [the longest x1 2.55 us: shards(): lax.all_to_all(grad_key, 'head', split_axis=0, concat_axis=1, tiled=True)]
  transfers between devices with their start and end apart: 11 -> 0, of which waited for: 9 -> 0; matrix products, arithmetic and copies ran while one was open for 27% -> 0% of each run, Pallas kernels for 0% -> 0%
where the time goes in v1:
time: 65.7 us; the launch traced here: 65.4 us
  Pallas kernels  58.2 us (89%)
  local copies, waits for them, and re-layouts  6.53 us (10%)
    pallas_call x1, Pallas kernels, shards(): pl.pallas_call(kernel, out_shape=[jax.ShapeDtypeStruct((128, PAIRS, 2, 12...  58.2 us
    unnamed x10, local copies, waits for them, and re-layouts  6.53 us

profile of v1, /device:TPU:1, one launch (start us, length us, event | category | flops | bytes accessed | tf_op | source)
XLA Modules:
  0.0 65.4 jit_solution(10636455699579374685)
XLA Ops:
  0.6 58.2 %shard_map.84 = (bf16[128,16,2,128]{3,2,1,0:T(2,128)(2,1)}, bf16[128,16,2,128]{3,2,1,0:T(2,128)(2,1)}, bf16[128,16,2,128]{3,2,1,0:T(2,128)(2,1)}, bf16[128,16,2,128]{3,2,1,0:T(2,128)(2,1)}) custom-call(bf16[32,128]{1,0:T(8,128)(2,1)} %bitcast.17, bf16[128,16,2,128]{3,2,1,0:T(2,128)(2,1)} %bitcast.13, bf16[128,16,2,128]{3,2,1,0:T(2,128)(2,1)} %bitcast.14, ...), custom_call_target="tpu_custom_call" | custom-call | tf_op jit(solution)/shard_map/pallas_call | solution.py:371
  58.9 0.0 copy-start.2
  58.9 2.4 %copy.13 = bf16[128,32,128]{2,1,0:T(8,128)(2,1)} copy(bf16[128,32,128]{2,1,0:T(8,128)(2,1)} %bitcast.12) | data formatting | bytes 2097152
  61.2 0.0 copy-done.2
  61.3 0.0 copy-start.1
  61.3 1.0 %copy.14 = bf16[128,32,128]{2,1,0:T(8,128)(2,1)} copy(bf16[128,32,128]{2,1,0:T(8,128)(2,1)S(1)} %bitcast.11) | data formatting | bytes 2097152
  62.2 0.6 copy-done.1
  62.9 0.0 copy-start
  62.9 1.0 %copy.15 = bf16[128,32,128]{2,1,0:T(8,128)(2,1)} copy(bf16[128,32,128]{2,1,0:T(8,128)(2,1)S(1)} %bitcast.10) | data formatting | bytes 2097152
  63.8 0.6 copy-done
  64.5 1.0 %copy.16 = bf16[128,32,128]{2,1,0:T(8,128)(2,1)} copy(bf16[128,32,128]{2,1,0:T(8,128)(2,1)S(1)} %bitcast.9) | data formatting | bytes 2097152
Async XLA Ops:
  58.9 2.4 %copy-start.2 = (bf16[128,16,2,128]{3,2,1,0:T(2,128)(2,1)S(1)}, bf16[128,16,2,128]{3,2,1,0:T(2,128)(2,1)}, u32[]{:S(2)}) copy-start(bf16[128,16,2,128]{3,2,1,0:T(2,128)(2,1)} %get-tuple-element.9) | copy-start | bytes 3145732
  61.3 1.6 %copy-start.1 = (bf16[128,16,2,128]{3,2,1,0:T(2,128)(2,1)S(1)}, bf16[128,16,2,128]{3,2,1,0:T(2,128)(2,1)}, u32[]{:S(2)}) copy-start(bf16[128,16,2,128]{3,2,1,0:T(2,128)(2,1)} %get-tuple-element.10) | copy-start | bytes 3145732
  62.9 1.6 %copy-start = (bf16[128,16,2,128]{3,2,1,0:T(2,128)(2,1)S(1)}, bf16[128,16,2,128]{3,2,1,0:T(2,128)(2,1)}, u32[]{:S(2)}) copy-start(bf16[128,16,2,128]{3,2,1,0:T(2,128)(2,1)} %get-tuple-element.11) | copy-start | bytes 3145732
